TPU v7x, 512 devices: a whole 4x8x8 slice. The times are simulated.
512 devices in a mesh: dp: 16 (over y, core), table: 32 (over x, z).
Axes of the slice: x: 4, y: 8, z: 8, core: 2. Of those that a mesh axis runs over, the one named last changes fastest.
Arguments:
- embedded: bfloat16 [2, 32768, 4096], P(None, 'dp', 'table'), may hold values from -1.1953125 to 1.1953125
- resid_grad: bfloat16 [2, 32768, 4096], P(None, 'dp', 'table'), may hold values from -0.29882812 to 0.29882812
- query_grad: bfloat16 [2, 32768, 2048], P(None, ('dp', 'table')), may hold values from -0.59765625 to 0.59765625
- query_weight: bfloat16 [4096, 2048], P('table'), may hold values from -0.09375 to 0.09375
- ngram_rows: int32 [2, 32768, 4], P(None, 'dp'), may hold values from 0 to 3199999, as said below
- touched_rows: int32 [32, 4, 12], replicated, may hold values from -1 to 3199999, as said below
- row_values: float32 [32, 4, 12, 1024], P('table'), may hold values from -6 to 6
- row_mean: float32 [32, 4, 12, 1024], P('table'), may hold values from -0.6 to 0.6
- row_square: float32 [32, 4, 12, 1024], P('table'), may hold values from 0.01 to 0.1
Outputs:
- weight_grad: float32 [4096, 2048], P('table')
- new_values: float32 [32, 4, 12, 1024], P('table')
- new_mean: float32 [32, 4, 12, 1024], P('table')
- new_square: float32 [32, 4, 12, 1024], P('table')
Inputs may be any that keep to these rules, and one draw needn't show every extreme that they name: `touched_rows`: owner o's list for slice s holds 1 to 12 distinct row ids of [o * 100000, (o + 1) * 100000) first, then -1; in every slice some owner's list is full. `ngram_rows`: every id of slice s is one of the listed rows of owner id // 100000 for slice s.
All inputs are finite; a program needn't handle non-finite values.
Results may differ from a plain program's by a relative error of at most 0.0003.
Values may be sent and summed in bfloat16 or wider, within the bound.
No kernel may reach another device: no remote copies, remote signals or barrier semaphores. Data moves between devices by JAX's collectives and lax.ppermute only.
A program may use at most 64 MiB of HBM per device.

v0:
```python
import jax
import jax.numpy as jnp
from jax import lax
from jax.sharding import PartitionSpec as P

SLICES = 4
SW = 1024
beta_one = 0.9
beta_two = 0.95
learn_rate = 0.01
adam_eps = 1e-08
adam_step = 10


def adam_rows(grads, values, mean, square, live):
    corr_one = 1.0 - beta_one**adam_step
    corr_two = 1.0 - beta_two**adam_step
    mean_next = beta_one * mean + (1.0 - beta_one) * grads
    square_next = beta_two * square + (1.0 - beta_two) * grads * grads
    update = learn_rate * (mean_next / corr_one) / (jnp.sqrt(square_next / corr_two) + adam_eps)
    values_next = values - update
    return (
        jnp.where(live, values_next, values),
        jnp.where(live, mean_next, mean),
        jnp.where(live, square_next, square),
    )


def make_step(emb_part, weight_part, carry, piece):
    back_part, wgrad = carry
    back = jnp.einsum("mrh,ph->mrp", piece, weight_part, preferred_element_type=jnp.float32)
    back_part = back
    wgrad = wgrad + jnp.einsum("mrp,mrh->ph", emb_part, piece, preferred_element_type=jnp.float32)
    return (back_part, wgrad)


def local(
    embedded,
    resid_grad,
    query_grad,
    query_weight,
    ngram_rows,
    touched_rows,
    row_values,
    row_mean,
    row_square,
):
    micro_count, group_tokens, width_part = embedded.shape
    hidden = query_grad.shape[2]
    tables = lax.axis_size("table")
    table_idx = lax.axis_index("table")
    zero_grad = jnp.zeros((width_part, hidden), jnp.float32)
    wgrad = zero_grad
    backs = []
    for micro in range(micro_count):
        start_back = jnp.zeros((1, group_tokens, width_part), jnp.float32)
        back_one, wgrad = make_step(
            embedded[micro : micro + 1],
            query_weight,
            (start_back, wgrad),
            lax.all_gather(query_grad[micro : micro + 1], "table", axis=1, tiled=True),
        )
        backs.append(back_one)
    back_all = jnp.concatenate(backs, axis=0)
    emb_grad = resid_grad.astype(jnp.float32) + back_all
    weight_grad = lax.psum(wgrad, "dp")
    slice_idx = table_idx * width_part // SW
    ids = lax.dynamic_index_in_dim(ngram_rows, slice_idx, 2, False)
    listed = lax.dynamic_index_in_dim(touched_rows, slice_idx, 1, False)
    entries = listed.shape[1]
    flat_list = listed.reshape(tables * entries)
    onehot = (ids[:, :, None] == flat_list[None, None, :]).astype(jnp.float32)
    buckets = jnp.einsum(
        "mtk,mtp->kp",
        onehot,
        emb_grad,
        precision=lax.Precision.HIGHEST,
        preferred_element_type=jnp.float32,
    )
    buckets = buckets.reshape(tables, entries, width_part)
    arrived = lax.all_to_all(buckets, "table", split_axis=0, concat_axis=0, tiled=True)
    per_slice = tables // SLICES
    local_grad = (
        arrived.reshape(SLICES, per_slice, entries, width_part)
        .transpose(0, 2, 1, 3)
        .reshape(SLICES, entries, per_slice * width_part)
    )
    mine = lax.dynamic_index_in_dim(touched_rows, table_idx, 0, False)
    live = (mine >= 0)[..., None]
    values = row_values[0]
    mean = row_mean[0]
    square = row_square[0]
    grads = lax.psum(local_grad, "dp")
    values_next, mean_next, square_next = adam_rows(grads, values, mean, square, live)
    return (weight_grad, values_next[None], mean_next[None], square_next[None])


def solution(mesh):
    placed = (
        P(None, "dp", "table"),
        P(None, "dp", "table"),
        P(None, ("dp", "table"), None),
        P("table", None),
        P(None, "dp", None),
        P(),
        P("table", None, None, None),
        P("table", None, None, None),
        P("table", None, None, None),
    )
    return jax.shard_map(
        local,
        mesh=mesh,
        in_specs=placed,
        out_specs=(
            P("table", None),
            P("table", None, None, None),
            P("table", None, None, None),
            P("table", None, None, None),
        ),
        check_vma=False,
    )
```

profile of v0, /device:TPU:25, one launch (start us, length us, event | category | flops | bytes accessed | tf_op | source)
XLA Modules:
  0.0 381.5 jit_solution(2230396503521548309)
XLA Ops:
  7.2 1.9 fusion.37
  9.2 0.7 all-gather.3.cloned.1.call-update
  9.9 0.9 constant_dynamic-slice_fusion.1
  10.8 0.8 constant_dynamic-slice_fusion
  11.6 0.1 copy.22
  11.7 0.1 eq.19
  11.8 107.7 %all-gather.5.cloned.1.call-done = bf16[1,2048,2048]{2,1,0:T(8,128)(2,1)} async-done(((bf16[1,64,2048]{2,1,0:T(8,128)(2,1)}), bf16[1,2048,2048]{2,1,0:T(8,128)(2,1)}) %all-gather.5.cloned.1.call-update) | async-done | bytes 8388624 | tf_op jit(solution)/shard_map/all_gather | solution.py:61
  119.5 6.7 %fusion.15 = f32[1,2048,128]{2,1,0:T(8,128)} fusion(bf16[128,2048]{1,0:T(8,128)(2,1)S(1)} %copy-done, bf16[1,2048,2048]{2,1,0:T(8,128)(2,1)} %all-gather.5.cloned.1.call-done), kind=kOutput, calls=%fused_computation.13 | convolution fusion | flops 1073741824 | bytes 9961472 | tf_op jit(solution)/shard_map/mrh,ph->mrp/dot_general | solution.py:31
  126.2 97.1 %all-gather.3.cloned.1.call-done = bf16[1,2048,2048]{2,1,0:T(8,128)(2,1)} async-done(((bf16[1,64,2048]{2,1,0:T(8,128)(2,1)}), bf16[1,2048,2048]{2,1,0:T(8,128)(2,1)}) %all-gather.3.cloned.1.call-update) | async-done | bytes 8388624 | tf_op jit(solution)/shard_map/all_gather | solution.py:61
  223.3 5.9 %fusion.12 = f32[1,2048,128]{2,1,0:T(8,128)S(1)} fusion(bf16[128,2048]{1,0:T(8,128)(2,1)S(1)} %copy-done, bf16[1,2048,2048]{2,1,0:T(8,128)(2,1)} %all-gather.3.cloned.1.call-done), kind=kOutput, calls=%fused_computation.12 | convolution fusion | flops 1073741824 | bytes 9961472 | tf_op jit(solution)/shard_map/mrh,ph->mrp/dot_general | solution.py:31
  229.2 3.1 fusion.24
  232.3 0.7 reshape.46
  233.0 5.2 %all-to-all-start = ((f32[32,12,128]{2,1,0:T(8,128)}), f32[32,12,128]{2,1,0:T(8,128)S(1)}, u32[]{:S(2)}, u32[]{:S(2)}) async-start(f32[32,12,128]{2,1,0:T(8,128)} %reshape.46), calls=%async_computation | async-start | bytes 524288 | tf_op jit(solution)/shard_map/all_to_all | solution.py:81
  238.1 0.2 all-reduce.3.cloned.1.call-start
  238.4 4.7 %fusion.2 = f32[128,2048]{1,0:T(8,128)S(1)} fusion(bf16[1,2048,2048]{2,1,0:T(8,128)(2,1)} %all-gather.5.cloned.1.call-done, bf16[2,2048,128]{2,1,0:T(8,128)(2,1)S(1)} %copy-done.1), kind=kOutput, calls=%fused_computation.2 | convolution fusion | flops 1073741824 | bytes 9961472 | tf_op jit(solution)/shard_map/mrp,mrh->ph/dot_general | solution.py:33
  243.1 5.7 %fusion.18 = f32[128,2048]{1,0:T(8,128)} fusion(f32[128,2048]{1,0:T(8,128)S(1)} %fusion.2, bf16[1,2048,2048]{2,1,0:T(8,128)(2,1)} %all-gather.3.cloned.1.call-done, bf16[2,2048,128]{2,1,0:T(8,128)(2,1)S(1)} %copy-done.1), kind=kOutput, calls=%fused_computation.14 | convolution fusion | flops 1074003968 | bytes 11010048 | tf_op jit(solution)/shard_map/mrp,mrh->ph/dot_general | solution.py:33
  248.8 0.1 copy.23
  248.9 0.7 reshape.48
  249.6 0.1 constant_dynamic-slice_fusion.2
  249.7 0.1 copy.25
  249.8 0.1 copy.21
  250.0 120.6 %all-reduce.3.cloned.1.call-done = (f32[128,2048]{1,0:T(8,128)}, f32[4,12,1024]{2,0,1:T(4,128)}) async-done(((f32[128,2048]{1,0:T(8,128)}, f32[4,12,1024]{2,0,1:T(4,128)}), (f32[128,2048]{1,0:T(8,128)}, f32[4,12,1024]{2,0,1:T(4,128)})) %all-reduce.3.cloned.1.call-update) | async-done | bytes 1245200 | tf_op jit(solution)/shard_map/psum | solution.py:66
  370.6 2.1 fusion.33
  372.7 2.3 copy.30
  (23 shorter events, 0.2 us)
Async XLA Ops:
  7.2 112.3 %copy-start = (bf16[128,2048]{1,0:T(8,128)(2,1)S(1)}, bf16[128,2048]{1,0:T(8,128)(2,1)}, u32[]{:S(2)}) copy-start(bf16[128,2048]{1,0:T(8,128)(2,1)} %param.12) | copy-start | bytes 1572868
  7.2 112.3 %all-gather.5.cloned.1.call-start = ((), (), s32[]{:S(2)}) async-start(), calls=%async_computation.2 | async-start | bytes 8650752 | tf_op jit(solution)/shard_map/all_gather | solution.py:61
  9.2 214.1 %all-gather.3.cloned.1.call-start = ((), (), s32[]{:S(2)}) async-start(), calls=%async_computation.1 | async-start | bytes 8650752 | tf_op jit(solution)/shard_map/all_gather | solution.py:61
  126.2 103.0 %copy-start.6 = (bf16[2,2048,128]{2,1,0:T(8,128)(2,1)S(1)}, bf16[2,2048,128]{2,1,0:T(8,128)(2,1)}, u32[]{:S(2)}) copy-start(bf16[2,2048,128]{2,1,0:T(8,128)(2,1)} %param.10) | copy-start | bytes 3145732
  126.2 112.2 %copy-start.1 = (bf16[2,2048,128]{2,1,0:T(8,128)(2,1)S(1)}, bf16[2,2048,128]{2,1,0:T(8,128)(2,1)}, u32[]{:S(2)}) copy-start(bf16[2,2048,128]{2,1,0:T(8,128)(2,1)} %param.9) | copy-start | bytes 3145732
  223.3 5.9 %copy-start.7 = (f32[1,2048,128]{2,1,0:T(8,128)S(1)}, f32[1,2048,128]{2,1,0:T(8,128)}, u32[]{:S(2)}) copy-start(f32[1,2048,128]{2,1,0:T(8,128)} %fusion.15) | copy-start | bytes 3145732
  233.0 15.8 %all-to-all-start = ((f32[32,12,128]{2,1,0:T(8,128)}), f32[32,12,128]{2,1,0:T(8,128)S(1)}, u32[]{:S(2)}, u32[]{:S(2)}) async-start(f32[32,12,128]{2,1,0:T(8,128)} %reshape.46), calls=%async_computation | async-start | bytes 524288 | tf_op jit(solution)/shard_map/all_to_all | solution.py:81
  238.1 132.4 %all-reduce.3.cloned.1.call-start = ((), (), s32[]{:S(2)}) async-start(), calls=%async_computation.3 | async-start | bytes 2490368 | tf_op jit(solution)/shard_map/psum | solution.py:66
  243.0 6.6 %copy-start.5 = (s32[32,4,12]{0,1,2:T(4,128)S(1)}, s32[32,4,12]{0,1,2:T(4,128)}, u32[]{:S(2)}) copy-start(s32[32,4,12]{0,1,2:T(4,128)} %param.14) | copy-start | bytes 18436
  243.1 127.5 %copy-start.2 = (f32[1,4,12,1024]{3,1,2,0:T(4,128)S(1)}, f32[1,4,12,1024]{3,1,2,0:T(4,128)}, u32[]{:S(2)}) copy-start(f32[1,4,12,1024]{3,1,2,0:T(4,128)} %param.17) | copy-start | bytes 589828
  243.1 127.5 %copy-start.3 = (f32[1,4,12,1024]{3,1,2,0:T(4,128)S(1)}, f32[1,4,12,1024]{3,1,2,0:T(4,128)}, u32[]{:S(2)}) copy-start(f32[1,4,12,1024]{3,1,2,0:T(4,128)} %param.16) | copy-start | bytes 589828
  243.1 127.5 %copy-start.4 = (f32[1,4,12,1024]{3,1,2,0:T(4,128)S(1)}, f32[1,4,12,1024]{3,1,2,0:T(4,128)}, u32[]{:S(2)}) copy-start(f32[1,4,12,1024]{3,1,2,0:T(4,128)} %param.15) | copy-start | bytes 589828
Sparse Core Ops, SparseCore 0:
  11.7 107.6 all-gather.4
  122.6 100.5 all-gather.2
  249.8 120.7 all-reduce.2
where the time goes:
time: 382 us
  waiting for transfers between devices  326 us (85%)
  matrix products  26 us (7%)
  between operations  13.9 us (4%)
  local copies, waits for them, and re-layouts  7.9 us (2%)
  starting transfers between devices  5.46 us (1%)
    all_gather x2, waiting for transfers between devices, local(): lax.all_gather(query_grad[micro:micro + 1], 'table', axis=1, tiled=True)  205 us
    psum x1, waiting for transfers between devices, local(): weight_grad = lax.psum(wgrad, 'dp')  121 us
    dot_general x2, matrix products, make_step(): jnp.einsum('mrh,ph->mrp', piece, weight_part, preferred_element_type=jnp....  12.6 us
    dot_general x2, matrix products, make_step(): jnp.einsum('mrp,mrh->ph', emb_part, piece, preferred_element_type=jnp.flo...  10.4 us
  transfers between devices with their start and end apart: 4, of which 3 were waited for; matrix products, arithmetic and copies ran while one was open for 5% of the time, Pallas kernels for 0%

commit v1 on v0

--- a/solution.py
+++ b/solution.py
@@ -63,7 +63,11 @@
         backs.append(back_one)
     back_all = jnp.concatenate(backs, axis=0)
     emb_grad = resid_grad.astype(jnp.float32) + back_all
-    weight_grad = lax.psum(wgrad, "dp")
+    weight_grad = wgrad
+    for hop in (1, 2, 4, 8):
+        weight_grad = weight_grad + lax.ppermute(
+            weight_grad, "dp", [(dev, dev ^ hop) for dev in range(16)]
+        )
     slice_idx = table_idx * width_part // SW
     ids = lax.dynamic_index_in_dim(ngram_rows, slice_idx, 2, False)
     listed = lax.dynamic_index_in_dim(touched_rows, slice_idx, 1, False)

time: 382 us -> 459 us (1.20)
  the two profiles are of different devices: /device:TPU:25 before, /device:TPU:1 now
where the time goes in v1:
time: 459 us
  waiting for transfers between devices  388 us (85%)
  matrix products  24.2 us (5%)
  starting transfers between devices  23.7 us (5%)
  between operations  14 us (3%)
  local copies, waits for them, and re-layouts  4.91 us (1%)
    all_gather x2, waiting for transfers between devices, local(): lax.all_gather(query_grad[micro:micro + 1], 'table', axis=1, tiled=True)  210 us
    psum x1, waiting for transfers between devices, local(): grads = lax.psum(local_grad, 'dp')  111 us
    ppermute x4, waiting for transfers between devices, local(): lax.ppermute(weight_grad, 'dp', [(dev, dev ^ hop) for dev in range(16)])  58 us
    ppermute x4, starting transfers between devices, local(): lax.ppermute(weight_grad, 'dp', [(dev, dev ^ hop) for dev in range(16)])  18.5 us
    dot_general x2, matrix products, make_step(): jnp.einsum('mrh,ph->mrp', piece, weight_part, preferred_element_type=jnp....  11.6 us
    dot_general x2, matrix products, make_step(): jnp.einsum('mrp,mrh->ph', emb_part, piece, preferred_element_type=jnp.flo...  9.5 us
    all_to_all x1, waiting for transfers between devices, local(): lax.all_to_all(buckets, 'table', split_axis=0, concat_axis=0, tiled=True)  9.44 us
  transfers between devices with their start and end apart: 8, of which 7 were waited for; matrix products, arithmetic and copies ran while one was open for 5% of the time, Pallas kernels for 0%

profile of v1, /device:TPU:1, one launch (start us, length us, event | category | flops | bytes accessed | tf_op | source)
XLA Modules:
  0.0 459.0 jit_solution(11360130986125192399)
XLA Ops:
  7.2 2.0 fusion.37
  9.3 0.7 all-gather.3.cloned.1.call-update
  10.0 110.0 %all-gather.5.cloned.1.call-done = bf16[1,2048,2048]{2,1,0:T(8,128)(2,1)} async-done(((bf16[1,64,2048]{2,1,0:T(8,128)(2,1)}), bf16[1,2048,2048]{2,1,0:T(8,128)(2,1)}) %all-gather.5.cloned.1.call-update) | async-done | bytes 8388624 | tf_op jit(solution)/shard_map/all_gather | solution.py:61
  120.0 4.8 %fusion.2 = f32[128,2048]{1,0:T(8,128)S(1)} fusion(bf16[1,2048,2048]{2,1,0:T(8,128)(2,1)} %all-gather.5.cloned.1.call-done, bf16[2,2048,128]{2,1,0:T(8,128)(2,1)} %param.9), kind=kOutput, calls=%fused_computation.2 | convolution fusion | flops 1073741824 | bytes 9961472 | tf_op jit(solution)/shard_map/mrp,mrh->ph/dot_general | solution.py:33
  124.8 99.5 %all-gather.3.cloned.1.call-done = bf16[1,2048,2048]{2,1,0:T(8,128)(2,1)} async-done(((bf16[1,64,2048]{2,1,0:T(8,128)(2,1)}), bf16[1,2048,2048]{2,1,0:T(8,128)(2,1)}) %all-gather.3.cloned.1.call-update) | async-done | bytes 8388624 | tf_op jit(solution)/shard_map/all_gather | solution.py:61
  224.4 4.7 %fusion.18 = f32[128,2048]{1,0:T(8,128)S(1)} fusion(f32[128,2048]{1,0:T(8,128)S(1)} %fusion.2, bf16[1,2048,2048]{2,1,0:T(8,128)(2,1)} %all-gather.3.cloned.1.call-done, bf16[2,2048,128]{2,1,0:T(8,128)(2,1)S(1)} %copy-done.1), kind=kOutput, calls=%fused_computation.14 | convolution fusion | flops 1074003968 | bytes 11010048 | tf_op jit(solution)/shard_map/mrp,mrh->ph/dot_general | solution.py:33
  229.0 3.3 collective-permute-start
  232.4 2.3 collective-permute-done
  234.8 3.1 collective-permute-start.1
  237.9 0.9 constant_dynamic-slice_fusion.1
  239.0 22.0 %collective-permute-done.1 = f32[128,2048]{1,0:T(8,128)S(1)} collective-permute-done((f32[128,2048]{1,0:T(8,128)S(1)}, f32[128,2048]{1,0:T(8,128)S(1)}, u32[]{:S(2)}, u32[]{:S(2)}) %collective-permute-start.1) | collective-permute-done | bytes 1048608 | tf_op jit(solution)/shard_map/ppermute | solution.py:68
  261.2 4.0 collective-permute-start.2
  265.2 5.8 %fusion.15 = f32[1,2048,128]{2,1,0:T(8,128)S(1)} fusion(bf16[128,2048]{1,0:T(8,128)(2,1)S(1)} %copy-done, bf16[1,2048,2048]{2,1,0:T(8,128)(2,1)} %all-gather.5.cloned.1.call-done), kind=kOutput, calls=%fused_computation.13 | convolution fusion | flops 1073741824 | bytes 9961472 | tf_op jit(solution)/shard_map/mrh,ph->mrp/dot_general | solution.py:31
  271.0 5.8 %fusion.12 = f32[1,2048,128]{2,1,0:T(8,128)S(1)} fusion(bf16[128,2048]{1,0:T(8,128)(2,1)S(1)} %copy-done, bf16[1,2048,2048]{2,1,0:T(8,128)(2,1)} %all-gather.3.cloned.1.call-done), kind=kOutput, calls=%fused_computation.12 | convolution fusion | flops 1073741824 | bytes 9961472 | tf_op jit(solution)/shard_map/mrh,ph->mrp/dot_general | solution.py:31
  276.9 33.7 %collective-permute-done.2 = f32[128,2048]{1,0:T(8,128)S(1)} collective-permute-done((f32[128,2048]{1,0:T(8,128)S(1)}, f32[128,2048]{1,0:T(8,128)S(1)}, u32[]{:S(2)}, u32[]{:S(2)}) %collective-permute-start.2) | collective-permute-done | bytes 1048608 | tf_op jit(solution)/shard_map/ppermute | solution.py:68
  310.7 8.0 %collective-permute-start.3 = (f32[128,2048]{1,0:T(8,128)S(1)}, f32[128,2048]{1,0:T(8,128)S(1)}, u32[]{:S(2)}, u32[]{:S(2)}) collective-permute-start(f32[128,2048]{1,0:T(8,128)S(1)} %add.46), channel_id=1, source_target_pairs={{0,256},{32,288},{64,320},{96,352},{128,384},{160,416},{192,448},{... | collective-permute-start | bytes 3145736 | tf_op jit(solution)/shard_map/ppermute | solution.py:68
  318.7 3.1 fusion.24
  321.8 0.7 reshape.46
  322.6 5.2 %all-to-all-start = ((f32[32,12,128]{2,1,0:T(8,128)}), f32[32,12,128]{2,1,0:T(8,128)S(1)}, u32[]{:S(2)}, u32[]{:S(2)}) async-start(f32[32,12,128]{2,1,0:T(8,128)} %reshape.46), calls=%async_computation | async-start | bytes 524288 | tf_op jit(solution)/shard_map/all_to_all | solution.py:85
  328.0 9.4 %all-to-all-done = f32[32,12,128]{2,1,0:T(8,128)S(1)} async-done(((f32[32,12,128]{2,1,0:T(8,128)}), f32[32,12,128]{2,1,0:T(8,128)S(1)}, u32[]{:S(2)}, u32[]{:S(2)}) %all-to-all-start) | async-done | bytes 196640 | tf_op jit(solution)/shard_map/all_to_all | solution.py:85
  337.5 0.7 reshape.48
  338.4 110.8 %all-reduce.2.cloned.1.call-done = f32[4,12,1024]{2,0,1:T(4,128)} async-done(((f32[4,12,1024]{2,0,1:T(4,128)}), f32[4,12,1024]{2,0,1:T(4,128)}) %all-reduce.2.cloned.1.call-update) | async-done | bytes 196624 | tf_op jit(solution)/shard_map/psum | solution.py:97
  449.2 2.2 fusion.33
  451.4 1.1 add.47
  (30 shorter events, 1.2 us)
Async XLA Ops:
  7.2 258.0 %copy-start = (bf16[128,2048]{1,0:T(8,128)(2,1)S(1)}, bf16[128,2048]{1,0:T(8,128)(2,1)}, u32[]{:S(2)}) copy-start(bf16[128,2048]{1,0:T(8,128)(2,1)} %param.12) | copy-start | bytes 1572868
  7.2 217.2 %copy-start.1 = (bf16[2,2048,128]{2,1,0:T(8,128)(2,1)S(1)}, bf16[2,2048,128]{2,1,0:T(8,128)(2,1)}, u32[]{:S(2)}) copy-start(bf16[2,2048,128]{2,1,0:T(8,128)(2,1)} %param.9) | copy-start | bytes 3145732
  7.2 112.8 %all-gather.5.cloned.1.call-start = ((), (), s32[]{:S(2)}) async-start(), calls=%async_computation.2 | async-start | bytes 8650752 | tf_op jit(solution)/shard_map/all_gather | solution.py:61
  9.2 215.1 %all-gather.3.cloned.1.call-start = ((), (), s32[]{:S(2)}) async-start(), calls=%async_computation.1 | async-start | bytes 8650752 | tf_op jit(solution)/shard_map/all_gather | solution.py:61
  124.8 114.0 %copy-start.4 = (s32[32,4,12]{0,1,2:T(4,128)S(1)}, s32[32,4,12]{0,1,2:T(4,128)}, u32[]{:S(2)}) copy-start(s32[32,4,12]{0,1,2:T(4,128)} %param.14) | copy-start | bytes 18436
  229.0 5.6 %collective-permute-start = (f32[128,2048]{1,0:T(8,128)S(1)}, f32[128,2048]{1,0:T(8,128)S(1)}, u32[]{:S(2)}, u32[]{:S(2)}) collective-permute-start(f32[128,2048]{1,0:T(8,128)S(1)} %fusion.18), channel_id=1, source_target_pairs={{0,32},{32,0},{64,96},{96,64},{128,160},{160,128},{192,224},{224,1... | collective-permute-start | bytes 3145736 | tf_op jit(solution)/shard_map/ppermute | solution.py:68
  234.8 26.2 %collective-permute-start.1 = (f32[128,2048]{1,0:T(8,128)S(1)}, f32[128,2048]{1,0:T(8,128)S(1)}, u32[]{:S(2)}, u32[]{:S(2)}) collective-permute-start(f32[128,2048]{1,0:T(8,128)S(1)} %add.44), channel_id=1, source_target_pairs={{0,64},{32,96},{64,0},{96,32},{128,192},{160,224},{192,128},{224,1... | collective-permute-start | bytes 3145736 | tf_op jit(solution)/shard_map/ppermute | solution.py:68
  261.2 49.4 %collective-permute-start.2 = (f32[128,2048]{1,0:T(8,128)S(1)}, f32[128,2048]{1,0:T(8,128)S(1)}, u32[]{:S(2)}, u32[]{:S(2)}) collective-permute-start(f32[128,2048]{1,0:T(8,128)S(1)} %add.45), channel_id=1, source_target_pairs={{0,128},{32,160},{64,192},{96,224},{128,0},{160,32},{192,64},{224,... | collective-permute-start | bytes 3145736 | tf_op jit(solution)/shard_map/ppermute | solution.py:68
  271.0 47.8 %copy-start.5 = (bf16[2,2048,128]{2,1,0:T(8,128)(2,1)S(1)}, bf16[2,2048,128]{2,1,0:T(8,128)(2,1)}, u32[]{:S(2)}) copy-start(bf16[2,2048,128]{2,1,0:T(8,128)(2,1)} %param.10) | copy-start | bytes 3145732
  276.8 172.3 %copy-start.2 = (f32[1,4,12,1024]{3,1,2,0:T(4,128)S(1)}, f32[1,4,12,1024]{3,1,2,0:T(4,128)}, u32[]{:S(2)}) copy-start(f32[1,4,12,1024]{3,1,2,0:T(4,128)} %param.17) | copy-start | bytes 589828
  276.9 172.3 %copy-start.3 = (f32[1,4,12,1024]{3,1,2,0:T(4,128)S(1)}, f32[1,4,12,1024]{3,1,2,0:T(4,128)}, u32[]{:S(2)}) copy-start(f32[1,4,12,1024]{3,1,2,0:T(4,128)} %param.16) | copy-start | bytes 589828
  310.7 140.7 %collective-permute-start.3 = (f32[128,2048]{1,0:T(8,128)S(1)}, f32[128,2048]{1,0:T(8,128)S(1)}, u32[]{:S(2)}, u32[]{:S(2)}) collective-permute-start(f32[128,2048]{1,0:T(8,128)S(1)} %add.46), channel_id=1, source_target_pairs={{0,256},{32,288},{64,320},{96,352},{128,384},{160,416},{192,448},{... | collective-permute-start | bytes 3145736 | tf_op jit(solution)/shard_map/ppermute | solution.py:68
  322.6 14.8 %all-to-all-start = ((f32[32,12,128]{2,1,0:T(8,128)}), f32[32,12,128]{2,1,0:T(8,128)S(1)}, u32[]{:S(2)}, u32[]{:S(2)}) async-start(f32[32,12,128]{2,1,0:T(8,128)} %reshape.46), calls=%async_computation | async-start | bytes 524288 | tf_op jit(solution)/shard_map/all_to_all | solution.py:85
  327.7 121.4 %all-reduce.2.cloned.1.call-start = ((), (), s32[]{:S(2)}) async-start(), calls=%async_computation.3 | async-start | bytes 393216 | tf_op jit(solution)/shard_map/psum | solution.py:97
Sparse Core Ops, SparseCore 0:
  11.2 108.7 all-gather.4
  123.7 100.5 all-gather.2
  338.4 110.7 all-reduce.1
